TPU v7x, 32 devices: a whole 2x2x4 slice. The times are simulated.
32 devices in a mesh: sub: 16 (over z, y, x), mode: 2 (over core).
Axes of the slice: x: 2, y: 2, z: 4, core: 2. Of those that a mesh axis runs over, the one named last changes fastest.
Arguments:
- coupling: bfloat16 [1024, 64, 128], P('sub'), may hold values from -0.5 to 0.5
- coupling_pairs: int32 [1024, 2], P('sub'), may hold values from 0 to 3, as said below
- modes: bfloat16 [1024, 256, 256], P('sub', None, 'mode'), may hold values from -6 to 6
- mode_weights: bfloat16 [1024, 256], P('sub', 'mode'), may hold values from 0 to 1, as said below
- parent_of: int32 [1024, 1], P('sub'), may hold values from 0 to 15; in each aligned block of 64 rows (0 to 63, 64 to 127, ...) at most 8 rows name the same one
- row_block: int32 [1024], P('sub'), may hold values from 0 to 7
- parent_modes: bfloat16 [16, 512, 256], P('sub'), may hold values from -1 to 1
- parent_eigs: float32 [16, 256], P('sub'), may hold values from 0.02 to 0.5
Outputs:
- strengths: float32 [1024, 256], P('sub', 'mode')
Inputs may be any that keep to these rules, and one draw needn't show every extreme that they name: `coupling_pairs`: within each child the 2 block indices are distinct. `parent_of`: the 64 children of one index of sub name any one parent at most 8 times; some parent is named exactly 8 times by some index's children. `mode_weights`: Positive.
All inputs are finite; a program needn't handle non-finite values.
Results may differ from a plain program's by a relative error of at most 0.0015.
Values may be sent and summed in bfloat16 or wider, within the bound.
A program may use at most 128 MiB of HBM per device.

v0:
```python
import jax
import jax.numpy as jnp
from jax import lax
from jax.sharding import PartitionSpec as P

M = 256
MP = 256
BLK = 64
CH_DEV = 64


def pick_blocks(modes, coupling_pairs):
    child_count, interface_rows, mode_cols = modes.shape
    blocks = modes.reshape(child_count, interface_rows // BLK, BLK, mode_cols)
    selector = (
        coupling_pairs[:, :, None]
        == jnp.arange(interface_rows // BLK, dtype=jnp.int32)[None, None, :]
    ).astype(jnp.bfloat16)
    picked = jnp.einsum(
        "skb,sbim->skim", selector, blocks, preferred_element_type=jnp.float32
    ).astype(jnp.bfloat16)
    return picked.reshape(child_count, coupling_pairs.shape[1] * BLK, mode_cols)


def weighted_records(coupling_rows, picked, weights):
    record = jnp.einsum("sij,sjm->sim", coupling_rows, picked, preferred_element_type=jnp.float32)
    return (record * weights[:, None, :].astype(jnp.float32)).astype(jnp.bfloat16)


def to_slots(values, slot_index, slot_count):
    empty = jnp.zeros((slot_count,) + values.shape[1:], values.dtype)
    return empty.at[slot_index].set(values)


def per_device(
    coupling, coupling_pairs, modes, mode_weights, parent_of, row_block, parent_modes, parent_eigs
):
    sub_count = lax.axis_size("sub")
    child_count = coupling.shape[0]
    mode_cols = modes.shape[2]
    capacity = max(2, 2 * child_count // sub_count)
    slot_count = sub_count * capacity
    owner = parent_of[:, 0]
    order_ids = jnp.arange(child_count, dtype=jnp.int32)
    earlier = (owner[:, None] == owner[None, :]) & (order_ids[None, :] < order_ids[:, None])
    position = jnp.sum(earlier.astype(jnp.int32), axis=1)
    slot_index = owner * capacity + position
    picked = pick_blocks(modes, coupling_pairs)
    row_send = to_slots(row_block, slot_index, slot_count).reshape(sub_count, capacity)
    record = weighted_records(coupling, picked, mode_weights)
    record_send = to_slots(record, slot_index, slot_count).reshape(
        sub_count, capacity, BLK, mode_cols
    )
    record_recv, row_recv = (
        lax.all_to_all(record_send, "sub", split_axis=0, concat_axis=0, tiled=True),
        lax.all_to_all(row_send, "sub", split_axis=0, concat_axis=0, tiled=True),
    )
    records = record_recv.reshape(slot_count, BLK, mode_cols)
    row_index = row_recv.reshape(slot_count)
    sep_blocks = parent_modes.shape[1] // BLK
    parent_blocks = parent_modes[0].reshape(sep_blocks, BLK, MP)
    group_size = min(64, slot_count)
    group_count = slot_count // group_size
    record_groups = records.reshape(group_count, group_size, BLK, mode_cols)
    row_groups = row_index.reshape(group_count, group_size)

    def project(gram_sum, members):
        record_part, row_part = members
        selector = (row_part[:, None] == jnp.arange(sep_blocks, dtype=jnp.int32)[None, :]).astype(
            jnp.bfloat16
        )
        parent_rows = jnp.einsum(
            "sb,bik->sik", selector, parent_blocks, preferred_element_type=jnp.float32
        ).astype(jnp.bfloat16)
        projected = jnp.einsum(
            "sik,sim->skm", parent_rows, record_part, preferred_element_type=jnp.float32
        ).astype(jnp.bfloat16)
        term = jnp.einsum("skm,slm->kl", projected, projected, preferred_element_type=jnp.float32)
        return (gram_sum + term, projected)

    gram_sum, projected_all = lax.scan(
        project, jnp.zeros((MP, MP), jnp.float32), (record_groups, row_groups)
    )
    gram_sum = lax.psum(gram_sum, "mode")
    pencil = jnp.diag(parent_eigs[0]) + gram_sum / (CH_DEV * M)
    factor = jnp.linalg.cholesky(pencil)
    identity = jnp.eye(MP, dtype=pencil.dtype)
    inverse = lax.linalg.triangular_solve(factor, identity, left_side=True, lower=True).astype(
        jnp.bfloat16
    )

    def strength(projected):
        rotated = jnp.einsum("kl,slm->skm", inverse, projected, preferred_element_type=jnp.float32)
        return jnp.sum(rotated * rotated, axis=1) / MP

    slot_values = lax.map(strength, projected_all).reshape(sub_count, capacity, mode_cols)
    returned = lax.all_to_all(slot_values, "sub", split_axis=0, concat_axis=0, tiled=True)
    return returned.reshape(slot_count, mode_cols)[slot_index]


def solution(mesh):
    in_specs = (
        P("sub", None, None),
        P("sub", None),
        P("sub", None, "mode"),
        P("sub", "mode"),
        P("sub", None),
        P("sub"),
        P("sub", None, None),
        P("sub", None),
    )
    out_specs = P("sub", "mode")
    return jax.shard_map(
        per_device, mesh=mesh, in_specs=in_specs, out_specs=out_specs, check_vma=False
    )
```

profile of v0, /device:TPU:0, one launch (start us, length us, event | category | flops | bytes accessed | tf_op | source)
XLA Modules:
  0.0 229.0 jit_solution(5430570650498612388)
XLA Ops:
  6.5 0.9 convert_reduce_fusion
  7.5 0.7 fusion.31
  8.1 0.9 scatter_custom_fusion
  9.1 0.7 all_to_all.12
  9.7 8.3 %all-to-all-start = ((s32[16,1,8]{2,1,0:T(1,128)}), s32[16,1,8]{2,1,0:T(1,128)S(1)}, u32[]{:S(2)}, u32[]{:S(2)}) async-start(s32[16,1,8]{2,1,0:T(1,128)} %bitcast.6), calls=%async_computation | async-start | bytes 16384 | tf_op jit(solution)/shard_map/all_to_all | solution.py:56
  18.1 0.8 copy.57
  18.9 5.6 %fusion.15 = bf16[64,2,64,128]{3,1,2,0:T(2,128)(2,1)S(1)} fusion(bf16[64,4,64,128]{3,2,1,0:T(8,128)(2,1)} %bitcast.113, s32[64,2]{1,0:T(8,128)S(1)} %copy.57), kind=kOutput, calls=%fused_computation.27 | convolution fusion | flops 9437696 | bytes 6291968 | tf_op jit(solution)/shard_map/skb,sbim->skim/dot_general | solution.py:19
  24.5 0.6 copy.59
  25.2 1.7 fusion.18
  26.9 0.5 broadcast_in_dim.55
  27.4 6.2 %scatter_fusion = bf16[128,64,128]{2,1,0:T(8,128)(2,1)S(1)} fusion(bf16[128,64,128]{2,1,0:T(8,128)(2,1)S(1)} %broadcast_in_dim.55, s32[64]{0:T(128)S(1)} %fusion.31, bf16[64,64,128]{2,1,0:T(8,128)(2,1)} %fusion.18), kind=kCustom, calls=%fused_computation.2 | custom fusion | bytes 3145984 | tf_op jit(solution)/shard_map/scatter | solution.py:32
  33.6 1.4 copy-done.1
  35.0 6.9 %all-to-all-start.1 = ((bf16[16,8,64,128]{3,2,1,0:T(8,128)(2,1)}), bf16[16,8,64,128]{3,2,1,0:T(8,128)(2,1)S(1)}, u32[]{:S(2)}, u32[]{:S(2)}) async-start(bf16[16,8,64,128]{3,2,1,0:T(8,128)(2,1)} %bitcast.107), calls=%async_computation.1 | async-start | bytes 4194304 | tf_op jit(solution)/shard_map/all_to_all | solution.py:55
  42.0 1.1 copy.60
  43.1 0.6 broadcast.151
  43.6 0.7 reduce.16
  44.4 40.2 %all-to-all-done.1 = bf16[16,8,64,128]{3,2,1,0:T(8,128)(2,1)S(1)} async-done(((bf16[16,8,64,128]{3,2,1,0:T(8,128)(2,1)}), bf16[16,8,64,128]{3,2,1,0:T(8,128)(2,1)S(1)}, u32[]{:S(2)}, u32[]{:S(2)}) %all-to-all-start.1) | async-done | bytes 2097184 | tf_op jit(solution)/shard_map/all_to_all | solution.py:55
  84.6 24.0 %while.26 = (s32[]{:T(128)}, f32[256,256]{1,0:T(8,128)}, bf16[2,64,256,128]{3,2,1,0:T(8,128)(2,1)}, s32[2,64]{1,0:T(2,128)S(1)}, bf16[8,64,256]{2,0,1:T(8,128)(2...) while((s32[]{:T(128)}, f32[256,256]{1,0:T(8,128)}, ...), condition=%wide.region_4.5_spmd.clone, body=%wide.region_3.4_spmd.clone.sunk | while | flops 1362231808 | bytes 18614116 | solution.py:81
  84.6 0.7 convolution_convert_fusion.4
  85.4 5.7 %bitcast_dynamic-update-slice_fusion.8 = (bf16[2,64,256,128]{3,2,1,0:T(8,128)(2,1)}, bf16[64,256,128]{2,1,0:T(8,128)(2,1)}) fusion(bf16[2,64,256,128]{3,2,1,0:T(8,128)(2,1)} %get-tuple-element.287, s32[]{:T(128)} %get-tuple-element.285, bf16[2,64,64,128]{3,2,1,0:T(8,128)(2,1)S(1)} %get-tuple-element.298, ...), kind=kOutput, calls=%fused_computation.11.clone.1 | convolution fusion | flops 270532608 | bytes 11535360 | tf_op jit(solution)/shard_map/while/body/eval_jaxpr/sik,sim->skm/dot_general | solution.py:75
  91.1 5.5 %fusion.62 = f32[256,256]{1,0:T(8,128)} fusion(bf16[64,256,128]{2,1,0:T(8,128)(2,1)} %get-tuple-element.275, f32[256,256]{1,0:T(8,128)} %get-tuple-element.286, pred[]{:T(512)S(6)} %compare.26), kind=kOutput, calls=%fused_computation.16.clone.1 | convolution fusion | flops 1073872896 | bytes 4718593 | tf_op jit(solution)/shard_map/while/body/eval_jaxpr/skm,slm->kl/dot_general | solution.py:78
  96.6 0.8 convolution_convert_fusion.4
  97.3 5.8 %bitcast_dynamic-update-slice_fusion.8 = (bf16[2,64,256,128]{3,2,1,0:T(8,128)(2,1)}, bf16[64,256,128]{2,1,0:T(8,128)(2,1)}) fusion(bf16[2,64,256,128]{3,2,1,0:T(8,128)(2,1)} %get-tuple-element.287, s32[]{:T(128)} %get-tuple-element.285, bf16[2,64,64,128]{3,2,1,0:T(8,128)(2,1)S(1)} %get-tuple-element.298, ...), kind=kOutput, calls=%fused_computation.11.clone.1 | convolution fusion | flops 270532608 | bytes 11535360 | tf_op jit(solution)/shard_map/while/body/eval_jaxpr/sik,sim->skm/dot_general | solution.py:75
  103.1 5.5 %fusion.62 = f32[256,256]{1,0:T(8,128)} fusion(bf16[64,256,128]{2,1,0:T(8,128)(2,1)} %get-tuple-element.275, f32[256,256]{1,0:T(8,128)} %get-tuple-element.286, pred[]{:T(512)S(6)} %compare.26), kind=kOutput, calls=%fused_computation.16.clone.1 | convolution fusion | flops 1073872896 | bytes 4718593 | tf_op jit(solution)/shard_map/while/body/eval_jaxpr/skm,slm->kl/dot_general | solution.py:78
  108.6 1.8 copy.61
  110.5 22.5 %all-reduce.3.cloned.1.call-done = f32[256,256]{0,1:T(8,128)} async-done(((f32[256,256]{0,1:T(8,128)}), f32[256,256]{0,1:T(8,128)}) %all-reduce.3.cloned.1.call-update) | async-done | bytes 262160 | tf_op jit(solution)/shard_map/psum | solution.py:84
  133.0 1.0 multiply_add_fusion
  134.1 1.0 fusion.19
  135.2 11.7 %cholesky.49 = f32[128,128]{1,0:T(8,128)S(1)} custom-call(f32[128,128]{1,0:T(8,128)S(1)} %cholesky.115), custom_call_target="Cholesky" | custom-call | tf_op jit(solution)/shard_map/jit(cholesky)/cholesky | solution.py:86
  146.9 9.8 %custom-call.14 = f32[1,128,128]{1,2,0:T(8,128)S(1)} custom-call(f32[1,128,128]{2,1,0:T(8,128)S(1)} %get-tuple-element.177), custom_call_target="InvertDiagBlocksLowerTriangular" | custom-call | tf_op jit(solution)/shard_map/jit(cholesky)/cholesky | solution.py:86
  157.2 11.7 %cholesky.103 = f32[128,128]{1,0:T(8,128)S(1)} custom-call(f32[128,128]{1,0:T(8,128)S(1)} %convolution_subtract_fusion.1), custom_call_target="Cholesky" | custom-call | tf_op jit(solution)/shard_map/jit(cholesky)/cholesky | solution.py:86
  169.3 0.7 compare_reduce_fusion
  171.3 4.0 %while.25 = (s32[]{:T(128)}, f32[256,256]{0,1:T(8,128)S(1)}, s32[2,2]{1,0:T(2,128)S(1)}, f32[2,128,128]{2,1,0:T(8,128)S(1)}, s32[]{:T(128)}) while((s32[]{:T(128)}, f32[256,256]{0,1:T(8,128)S(1)}, s32[2,2]{1,0:T(2,128)S(1)}, f32[2,128,128]{2,1,0:T(8,128)S(1)}, s32[]{:T(128)}) %tuple.70), condition=%wide.while_cond, body=%wide.while_body.sunk | while | flops 2 | bytes 393321 | solution.py:88
  171.3 0.6 fusion.56
  171.8 1.3 dynamic-slice.7
  173.3 0.6 fusion.56
  173.8 1.3 dynamic-slice.7
  175.3 19.9 %custom-call.15 = f32[2,128,128]{1,2,0:T(8,128)S(1)} custom-call(f32[2,128,128]{2,1,0:T(8,128)S(1)} %get-tuple-element.70), custom_call_target="InvertDiagBlocksLowerTriangular" | custom-call | tf_op jit(solution)/shard_map/triangular_solve | solution.py:88
  195.4 0.4 convolution_subtract_fusion
  195.8 0.3 convolution_convert_fusion.2
  196.2 10.5 %while.24 = (s32[]{:T(128)}, f32[2,64,128]{2,1,0:T(8,128)}, bf16[2,64,256,128]{3,2,1,0:T(8,128)(2,1)}, bf16[256,256]{1,0:T(8,128)(2,1)S(1)}, s32[]{:T(128)}) while((s32[]{:T(128)}, f32[2,64,128]{2,1,0:T(8,128)}, bf16[2,64,256,128]{3,2,1,0:T(8,128)(2,1)}, bf16[256,256]{1,0:T(8,128)(2,1)S(1)}, s32[]{:T(128)}) %tuple.73), condition=%wide.region_12.13_spmd, body=%wide.region_10.12_spmd.sunk | while | flops 1077936128 | bytes 4424765 | solution.py:96
  196.2 4.6 %multiply_reduce_fusion.2 = f32[64,128]{1,0:T(8,128)S(1)} fusion(bf16[2,64,256,128]{3,2,1,0:T(8,128)(2,1)} %get-tuple-element.328, s32[]{:T(128)} %get-tuple-element.321, bf16[256,256]{1,0:T(8,128)(2,1)S(1)} %get-tuple-element.329), kind=kOutput, calls=%fused_computation.3.clone.1 | convolution fusion | flops 1077927936 | bytes 4358656 | tf_op jit(solution)/shard_map/while/body/eval_jaxpr/kl,slm->skm/dot_general | solution.py:93
  200.8 0.6 bitcast_dynamic-update-slice_fusion.6
  201.4 4.6 %multiply_reduce_fusion.2 = f32[64,128]{1,0:T(8,128)S(1)} fusion(bf16[2,64,256,128]{3,2,1,0:T(8,128)(2,1)} %get-tuple-element.328, s32[]{:T(128)} %get-tuple-element.321, bf16[256,256]{1,0:T(8,128)(2,1)S(1)} %get-tuple-element.329), kind=kOutput, calls=%fused_computation.3.clone.1 | convolution fusion | flops 1077927936 | bytes 4358656 | tf_op jit(solution)/shard_map/while/body/eval_jaxpr/kl,slm->skm/dot_general | solution.py:93
  206.0 0.6 bitcast_dynamic-update-slice_fusion.6
  206.6 6.8 %all-to-all-start.2 = ((f32[16,8,128]{2,1,0:T(8,128)}), f32[16,8,128]{2,1,0:T(8,128)S(1)}, u32[]{:S(2)}, u32[]{:S(2)}) async-start(f32[16,8,128]{2,1,0:T(8,128)} %bitcast.21), calls=%async_computation.2 | async-start | bytes 131072 | tf_op jit(solution)/shard_map/all_to_all | solution.py:97
  213.5 7.5 %all-to-all-done.2 = f32[16,8,128]{2,1,0:T(8,128)S(1)} async-done(((f32[16,8,128]{2,1,0:T(8,128)}), f32[16,8,128]{2,1,0:T(8,128)S(1)}, u32[]{:S(2)}, u32[]{:S(2)}) %all-to-all-start.2) | async-done | bytes 65568 | tf_op jit(solution)/shard_map/all_to_all | solution.py:97
  221.0 1.2 gather_fusion
  (43 shorter events, 1.9 us)
Async XLA Ops:
  6.5 18.6 %copy-start = (bf16[64,64,128]{2,1,0:T(8,128)(2,1)S(1)}, bf16[64,64,128]{2,1,0:T(8,128)(2,1)}, u32[]{:S(2)}) copy-start(bf16[64,64,128]{2,1,0:T(8,128)(2,1)} %param.12) | copy-start | bytes 3145732
  9.7 23.8 %all-to-all-start = ((s32[16,1,8]{2,1,0:T(1,128)}), s32[16,1,8]{2,1,0:T(1,128)S(1)}, u32[]{:S(2)}, u32[]{:S(2)}) async-start(s32[16,1,8]{2,1,0:T(1,128)} %bitcast.6), calls=%async_computation | async-start | bytes 16384 | tf_op jit(solution)/shard_map/all_to_all | solution.py:56
  24.5 0.7 copy-start.2
  33.6 1.4 copy-start.1
  35.0 49.6 %all-to-all-start.1 = ((bf16[16,8,64,128]{3,2,1,0:T(8,128)(2,1)}), bf16[16,8,64,128]{3,2,1,0:T(8,128)(2,1)S(1)}, u32[]{:S(2)}, u32[]{:S(2)}) async-start(bf16[16,8,64,128]{3,2,1,0:T(8,128)(2,1)} %bitcast.107), calls=%async_computation.1 | async-start | bytes 4194304 | tf_op jit(solution)/shard_map/all_to_all | solution.py:55
  41.9 91.1 %all-reduce.3.cloned.1.call-start = ((), (), s32[]{:S(2)}) async-start(), calls=%async_computation.3 | async-start | bytes 524288 | tf_op jit(solution)/shard_map/psum | solution.py:84
  84.6 48.4 %copy-start.3 = (f32[1,256]{1,0:T(1,128)S(1)}, f32[1,256]{1,0:T(1,128)}, u32[]{:S(2)}) copy-start(f32[1,256]{1,0:T(1,128)} %param.19) | copy-start | bytes 3076
  206.6 14.4 %all-to-all-start.2 = ((f32[16,8,128]{2,1,0:T(8,128)}), f32[16,8,128]{2,1,0:T(8,128)S(1)}, u32[]{:S(2)}, u32[]{:S(2)}) async-start(f32[16,8,128]{2,1,0:T(8,128)} %bitcast.21), calls=%async_computation.2 | async-start | bytes 131072 | tf_op jit(solution)/shard_map/all_to_all | solution.py:97
Sparse Core Ops, SparseCore 0:
  110.5 22.4 all-reduce.2
where the time goes:
time: 230 us; the launch traced here: 229 us
  waiting for transfers between devices  70.3 us (31%)
  other arithmetic  59.4 us (26%)
  matrix products  41.9 us (18%)
  starting transfers between devices  22.1 us (10%)
  local copies, waits for them, and re-layouts  20.3 us (9%)
  between operations  14.9 us (6%)
    all_to_all x1, waiting for transfers between devices, per_device(): lax.all_to_all(record_send, 'sub', split_axis=0, concat_axis=0, tiled=True)  40.2 us
    another operation x6, other arithmetic, per_device(): factor = jnp.linalg.cholesky(pencil)  34 us
    psum x1, waiting for transfers between devices, per_device(): gram_sum = lax.psum(gram_sum, 'mode')  22.5 us
    another operation x4, other arithmetic, per_device(): lax.linalg.triangular_solve(factor, identity, left_side=True, lower=True)  19.9 us
    dot_general x2, matrix products, project(): jnp.einsum('sik,sim->skm', parent_rows, record_part, preferred_element_ty...  11.5 us
    dot_general x2, matrix products, project(): jnp.einsum('skm,slm->kl', projected, projected, preferred_element_type=jn...  11 us
    dot_general x2, matrix products, strength(): jnp.einsum('kl,slm->skm', inverse, projected, preferred_element_type=jnp....  9.22 us
    all_to_all x1, starting transfers between devices, per_device(): lax.all_to_all(row_send, 'sub', split_axis=0, concat_axis=0, tiled=True)  8.34 us
  transfers between devices with their start and end apart: 4, of which 3 were waited for; matrix products, arithmetic and copies ran while one was open for 8% of the time, Pallas kernels for 0%

commit v1 on v0

--- a/solution.py
+++ b/solution.py
@@ -81,7 +81,12 @@
     gram_sum, projected_all = lax.scan(
         project, jnp.zeros((MP, MP), jnp.float32), (record_groups, row_groups)
     )
-    gram_sum = lax.psum(gram_sum, "mode")
+
+    def guide_the_works(block_here):
+        h_now = jnp.sum(lax.all_gather(block_here, "mode"), axis=0)
+        return h_now
+
+    gram_sum = guide_the_works(gram_sum)
     pencil = jnp.diag(parent_eigs[0]) + gram_sum / (CH_DEV * M)
     factor = jnp.linalg.cholesky(pencil)
     identity = jnp.eye(MP, dtype=pencil.dtype)

time: 230 us -> 198 us (0.86)
  waiting for transfers between devices: 70.3 us -> 47.7 us
  between operations: 14.9 us -> 1.55 us
  starting transfers between devices: 22.1 us -> 25.1 us
  blocking collectives: 0 us -> 2.56 us
    psum x1 -> x0, waiting for transfers between devices: 22.5 us -> none  [per_device(): gram_sum = lax.psum(gram_sum, 'mode')]
    all_to_all x1, starting transfers between devices: 6.83 us -> 9.83 us  [per_device(): lax.all_to_all(slot_values, 'sub', split_axis=0, concat_axis=0, tiled=True)]
    all_gather x0 -> x1, blocking collectives: none -> 2.56 us  [guide_the_works(): h_now = jnp.sum(lax.all_gather(block_here, 'mode'), axis=0)]
  transfers between devices with their start and end apart: 4 -> 3, of which waited for: 3 -> 2; matrix products, arithmetic and copies ran while one was open for 8% -> 9% of each run, Pallas kernels for 0% -> 0%
where the time goes in v1:
time: 198 us; the launch traced here: 197 us
  other arithmetic  58.2 us (29%)
  waiting for transfers between devices  47.7 us (24%)
  matrix products  41.9 us (21%)
  starting transfers between devices  25.1 us (13%)
  local copies, waits for them, and re-layouts  20.1 us (10%)
  blocking collectives  2.56 us (1%)
    all_to_all x1, waiting for transfers between devices, per_device(): lax.all_to_all(record_send, 'sub', split_axis=0, concat_axis=0, tiled=True)  40.2 us
    another operation x6, other arithmetic, per_device(): factor = jnp.linalg.cholesky(pencil)  33.9 us
    another operation x4, other arithmetic, per_device(): lax.linalg.triangular_solve(factor, identity, left_side=True, lower=True)  20.5 us
    dot_general x2, matrix products, project(): jnp.einsum('sik,sim->skm', parent_rows, record_part, preferred_element_ty...  11.5 us
    dot_general x2, matrix products, project(): jnp.einsum('skm,slm->kl', projected, projected, preferred_element_type=jn...  11 us
    all_to_all x1, starting transfers between devices, per_device(): lax.all_to_all(slot_values, 'sub', split_axis=0, concat_axis=0, tiled=True)  9.83 us
    dot_general x2, matrix products, strength(): jnp.einsum('kl,slm->skm', inverse, projected, preferred_element_type=jnp....  9.22 us
    all_to_all x1, starting transfers between devices, per_device(): lax.all_to_all(row_send, 'sub', split_axis=0, concat_axis=0, tiled=True)  8.34 us
  transfers between devices with their start and end apart: 3, of which 2 were waited for; matrix products, arithmetic and copies ran while one was open for 9% of the time, Pallas kernels for 0%

profile of v1, /device:TPU:0, one launch (start us, length us, event | category | flops | bytes accessed | tf_op | source)
XLA Modules:
  0.0 197.4 jit_solution(18015423203249322042)
XLA Ops:
  0.0 0.9 convert_reduce_fusion
  0.9 0.7 fusion.33
  1.6 0.9 scatter_custom_fusion
  2.5 0.7 all_to_all.12
  3.2 8.3 %all-to-all-start = ((s32[16,1,8]{2,1,0:T(1,128)}), s32[16,1,8]{2,1,0:T(1,128)S(1)}, u32[]{:S(2)}, u32[]{:S(2)}) async-start(s32[16,1,8]{2,1,0:T(1,128)} %bitcast.6), calls=%async_computation | async-start | bytes 16384 | tf_op jit(solution)/shard_map/all_to_all | solution.py:56
  11.6 0.8 copy.59
  12.3 5.6 %fusion.15 = bf16[64,2,64,128]{3,1,2,0:T(2,128)(2,1)S(1)} fusion(bf16[64,4,64,128]{3,2,1,0:T(8,128)(2,1)} %bitcast.116, s32[64,2]{1,0:T(8,128)S(1)} %copy.59), kind=kOutput, calls=%fused_computation.27 | convolution fusion | flops 9437696 | bytes 6291968 | tf_op jit(solution)/shard_map/skb,sbim->skim/dot_general | solution.py:19
  17.9 0.6 copy.61
  18.6 1.7 fusion.18
  20.3 0.5 broadcast_in_dim.57
  20.9 6.2 %scatter_fusion = bf16[128,64,128]{2,1,0:T(8,128)(2,1)S(1)} fusion(bf16[128,64,128]{2,1,0:T(8,128)(2,1)S(1)} %broadcast_in_dim.57, s32[64]{0:T(128)S(1)} %fusion.33, bf16[64,64,128]{2,1,0:T(8,128)(2,1)} %fusion.18), kind=kCustom, calls=%fused_computation.2 | custom fusion | bytes 3145984 | tf_op jit(solution)/shard_map/scatter | solution.py:32
  27.1 1.4 copy-done.1
  28.4 6.9 %all-to-all-start.1 = ((bf16[16,8,64,128]{3,2,1,0:T(8,128)(2,1)}), bf16[16,8,64,128]{3,2,1,0:T(8,128)(2,1)S(1)}, u32[]{:S(2)}, u32[]{:S(2)}) async-start(bf16[16,8,64,128]{3,2,1,0:T(8,128)(2,1)} %bitcast.110), calls=%async_computation.1 | async-start | bytes 4194304 | tf_op jit(solution)/shard_map/all_to_all | solution.py:55
  35.4 1.1 copy.62
  36.5 0.6 broadcast.156
  37.1 0.7 reduce.16
  37.9 40.2 %all-to-all-done.1 = bf16[16,8,64,128]{3,2,1,0:T(8,128)(2,1)S(1)} async-done(((bf16[16,8,64,128]{3,2,1,0:T(8,128)(2,1)}), bf16[16,8,64,128]{3,2,1,0:T(8,128)(2,1)S(1)}, u32[]{:S(2)}, u32[]{:S(2)}) %all-to-all-start.1) | async-done | bytes 2097184 | tf_op jit(solution)/shard_map/all_to_all | solution.py:55
  78.1 24.0 %while.26 = (s32[]{:T(128)}, f32[256,256]{1,0:T(8,128)}, bf16[2,64,256,128]{3,2,1,0:T(8,128)(2,1)}, s32[2,64]{1,0:T(2,128)S(1)}, bf16[8,64,256]{2,0,1:T(8,128)(2...) while((s32[]{:T(128)}, f32[256,256]{1,0:T(8,128)}, ...), condition=%wide.region_4.5_spmd.clone, body=%wide.region_3.4_spmd.clone.sunk | while | flops 1362231808 | bytes 18614116 | solution.py:81
  78.1 0.7 convolution_convert_fusion.4
  78.8 5.7 %bitcast_dynamic-update-slice_fusion.8 = (bf16[2,64,256,128]{3,2,1,0:T(8,128)(2,1)}, bf16[64,256,128]{2,1,0:T(8,128)(2,1)}) fusion(bf16[2,64,256,128]{3,2,1,0:T(8,128)(2,1)} %get-tuple-element.289, s32[]{:T(128)} %get-tuple-element.287, bf16[2,64,64,128]{3,2,1,0:T(8,128)(2,1)S(1)} %get-tuple-element.300, ...), kind=kOutput, calls=%fused_computation.11.clone.1 | convolution fusion | flops 270532608 | bytes 11535360 | tf_op jit(solution)/shard_map/while/body/eval_jaxpr/sik,sim->skm/dot_general | solution.py:75
  84.6 5.5 %fusion.64 = f32[256,256]{1,0:T(8,128)} fusion(bf16[64,256,128]{2,1,0:T(8,128)(2,1)} %get-tuple-element.277, f32[256,256]{1,0:T(8,128)} %get-tuple-element.288, pred[]{:T(512)S(6)} %compare.26), kind=kOutput, calls=%fused_computation.16.clone.1 | convolution fusion | flops 1073872896 | bytes 4718593 | tf_op jit(solution)/shard_map/while/body/eval_jaxpr/skm,slm->kl/dot_general | solution.py:78
  90.0 0.8 convolution_convert_fusion.4
  90.8 5.8 %bitcast_dynamic-update-slice_fusion.8 = (bf16[2,64,256,128]{3,2,1,0:T(8,128)(2,1)}, bf16[64,256,128]{2,1,0:T(8,128)(2,1)}) fusion(bf16[2,64,256,128]{3,2,1,0:T(8,128)(2,1)} %get-tuple-element.289, s32[]{:T(128)} %get-tuple-element.287, bf16[2,64,64,128]{3,2,1,0:T(8,128)(2,1)S(1)} %get-tuple-element.300, ...), kind=kOutput, calls=%fused_computation.11.clone.1 | convolution fusion | flops 270532608 | bytes 11535360 | tf_op jit(solution)/shard_map/while/body/eval_jaxpr/sik,sim->skm/dot_general | solution.py:75
  96.6 5.5 %fusion.64 = f32[256,256]{1,0:T(8,128)} fusion(bf16[64,256,128]{2,1,0:T(8,128)(2,1)} %get-tuple-element.277, f32[256,256]{1,0:T(8,128)} %get-tuple-element.288, pred[]{:T(512)S(6)} %compare.26), kind=kOutput, calls=%fused_computation.16.clone.1 | convolution fusion | flops 1073872896 | bytes 4718593 | tf_op jit(solution)/shard_map/while/body/eval_jaxpr/skm,slm->kl/dot_general | solution.py:78
  102.1 2.6 %all-gather = f32[512,256]{1,0:T(8,128)S(1)} all-gather(f32[256,256]{1,0:T(8,128)} %get-tuple-element.61), channel_id=2, replica_groups=mesh['sub'=16,'mode'=2] {'mode'}, dimensions={0}, use_global_device_ids=true | all-gather | bytes 786432 | tf_op jit(solution)/shard_map/all_gather | solution.py:86
  105.3 11.7 %cholesky.49 = f32[128,128]{1,0:T(8,128)S(1)} custom-call(f32[128,128]{1,0:T(8,128)S(1)} %cholesky.115), custom_call_target="Cholesky" | custom-call | tf_op jit(solution)/shard_map/jit(cholesky)/cholesky | solution.py:91
  117.0 9.8 %custom-call.14 = f32[1,128,128]{1,2,0:T(8,128)S(1)} custom-call(f32[1,128,128]{2,1,0:T(8,128)S(1)} %get-tuple-element.177), custom_call_target="InvertDiagBlocksLowerTriangular" | custom-call | tf_op jit(solution)/shard_map/jit(cholesky)/cholesky | solution.py:91
  127.0 0.3 convolution_subtract_fusion.1
  127.3 11.7 %cholesky.103 = f32[128,128]{1,0:T(8,128)S(1)} custom-call(f32[128,128]{1,0:T(8,128)S(1)} %convolution_subtract_fusion.1), custom_call_target="Cholesky" | custom-call | tf_op jit(solution)/shard_map/jit(cholesky)/cholesky | solution.py:91
  139.4 0.6 compare_reduce_fusion
  141.4 5.4 %while.25 = (s32[]{:T(128)}, f32[256,256]{0,1:T(8,128)S(1)}, s32[2,2]{1,0:T(2,128)S(1)}, f32[2,128,128]{2,1,0:T(8,128)}, s32[]{:T(128)}) while((s32[]{:T(128)}, f32[256,256]{0,1:T(8,128)S(1)}, s32[2,2]{1,0:T(2,128)S(1)}, f32[2,128,128]{2,1,0:T(8,128)}, s32[]{:T(128)}) %tuple.71), condition=%wide.while_cond, body=%wide.while_body.sunk | while | flops 2 | bytes 393829 | solution.py:93
  141.6 0.6 fusion.58
  142.2 1.3 dynamic-slice.7
  143.6 0.6 bitcast_dynamic-update-slice_fusion.7
  144.2 0.6 fusion.58
  144.8 1.3 dynamic-slice.7
  146.2 0.6 bitcast_dynamic-update-slice_fusion.7
  146.8 20.5 %custom-call.15 = f32[2,128,128]{1,2,0:T(8,128)S(1)} custom-call(f32[2,128,128]{2,1,0:T(8,128)} %get-tuple-element.70), custom_call_target="InvertDiagBlocksLowerTriangular" | custom-call | tf_op jit(solution)/shard_map/triangular_solve | solution.py:93
  167.6 0.4 convolution_subtract_fusion
  168.0 0.3 convolution_convert_fusion.2
  168.3 10.5 %while.24 = (s32[]{:T(128)}, f32[2,64,128]{2,1,0:T(8,128)}, bf16[2,64,256,128]{3,2,1,0:T(8,128)(2,1)}, bf16[256,256]{1,0:T(8,128)(2,1)S(1)}, s32[]{:T(128)}) while((s32[]{:T(128)}, f32[2,64,128]{2,1,0:T(8,128)}, bf16[2,64,256,128]{3,2,1,0:T(8,128)(2,1)}, bf16[256,256]{1,0:T(8,128)(2,1)S(1)}, s32[]{:T(128)}) %tuple.74), condition=%wide.region_12.13_spmd, body=%wide.region_10.12_spmd.sunk | while | flops 1077936128 | bytes 4424765 | solution.py:101
  168.3 4.6 %multiply_reduce_fusion.2 = f32[64,128]{1,0:T(8,128)S(1)} fusion(bf16[2,64,256,128]{3,2,1,0:T(8,128)(2,1)} %get-tuple-element.330, s32[]{:T(128)} %get-tuple-element.323, bf16[256,256]{1,0:T(8,128)(2,1)S(1)} %get-tuple-element.331), kind=kOutput, calls=%fused_computation.3.clone.1 | convolution fusion | flops 1077927936 | bytes 4358656 | tf_op jit(solution)/shard_map/while/body/eval_jaxpr/kl,slm->skm/dot_general | solution.py:98
  172.9 0.6 bitcast_dynamic-update-slice_fusion.6
  173.6 4.6 %multiply_reduce_fusion.2 = f32[64,128]{1,0:T(8,128)S(1)} fusion(bf16[2,64,256,128]{3,2,1,0:T(8,128)(2,1)} %get-tuple-element.330, s32[]{:T(128)} %get-tuple-element.323, bf16[256,256]{1,0:T(8,128)(2,1)S(1)} %get-tuple-element.331), kind=kOutput, calls=%fused_computation.3.clone.1 | convolution fusion | flops 1077927936 | bytes 4358656 | tf_op jit(solution)/shard_map/while/body/eval_jaxpr/kl,slm->skm/dot_general | solution.py:98
  178.2 0.6 bitcast_dynamic-update-slice_fusion.6
  178.8 9.8 %all-to-all-start.2 = ((f32[16,8,128]{2,1,0:T(8,128)}), f32[16,8,128]{2,1,0:T(8,128)S(1)}, u32[]{:S(2)}, u32[]{:S(2)}) async-start(f32[16,8,128]{2,1,0:T(8,128)} %bitcast.22), calls=%async_computation.2 | async-start | bytes 131072 | tf_op jit(solution)/shard_map/all_to_all | solution.py:102
  188.6 7.5 %all-to-all-done.2 = f32[16,8,128]{2,1,0:T(8,128)S(1)} async-done(((f32[16,8,128]{2,1,0:T(8,128)}), f32[16,8,128]{2,1,0:T(8,128)S(1)}, u32[]{:S(2)}, u32[]{:S(2)}) %all-to-all-start.2) | async-done | bytes 65568 | tf_op jit(solution)/shard_map/all_to_all | solution.py:102
  196.2 1.2 gather_fusion
  (43 shorter events, 2.0 us)
Async XLA Ops:
  0.0 18.6 %copy-start = (bf16[64,64,128]{2,1,0:T(8,128)(2,1)S(1)}, bf16[64,64,128]{2,1,0:T(8,128)(2,1)}, u32[]{:S(2)}) copy-start(bf16[64,64,128]{2,1,0:T(8,128)(2,1)} %param.12) | copy-start | bytes 3145732
  3.2 23.8 %all-to-all-start = ((s32[16,1,8]{2,1,0:T(1,128)}), s32[16,1,8]{2,1,0:T(1,128)S(1)}, u32[]{:S(2)}, u32[]{:S(2)}) async-start(s32[16,1,8]{2,1,0:T(1,128)} %bitcast.6), calls=%async_computation | async-start | bytes 16384 | tf_op jit(solution)/shard_map/all_to_all | solution.py:56
  17.9 0.7 copy-start.2
  27.0 1.4 copy-start.1
  28.4 49.6 %all-to-all-start.1 = ((bf16[16,8,64,128]{3,2,1,0:T(8,128)(2,1)}), bf16[16,8,64,128]{3,2,1,0:T(8,128)(2,1)S(1)}, u32[]{:S(2)}, u32[]{:S(2)}) async-start(bf16[16,8,64,128]{3,2,1,0:T(8,128)(2,1)} %bitcast.110), calls=%async_computation.1 | async-start | bytes 4194304 | tf_op jit(solution)/shard_map/all_to_all | solution.py:55
  78.1 26.7 %copy-start.3 = (f32[1,256]{1,0:T(1,128)S(1)}, f32[1,256]{1,0:T(1,128)}, u32[]{:S(2)}) copy-start(f32[1,256]{1,0:T(1,128)} %param.19) | copy-start | bytes 3076
  178.8 17.4 %all-to-all-start.2 = ((f32[16,8,128]{2,1,0:T(8,128)}), f32[16,8,128]{2,1,0:T(8,128)S(1)}, u32[]{:S(2)}, u32[]{:S(2)}) async-start(f32[16,8,128]{2,1,0:T(8,128)} %bitcast.22), calls=%async_computation.2 | async-start | bytes 131072 | tf_op jit(solution)/shard_map/all_to_all | solution.py:102
